TPU v7x, 512 devices: a whole 4x8x8 slice. The times are simulated.
512 devices in a mesh: space: 32 (over y, z_lo), mode: 16 (over z_hi, x, core).
Axes of the slice: x: 4, y: 8, z: 8 (z_hi: 2, z_lo: 4; z = z_hi * 4 + z_lo), core: 2. Of those that a mesh axis runs over, the one named last changes fastest.
Arguments:
- left_modes: bfloat16 [2, 12, 4096, 4096], P(None, None, 'space', 'mode'), may hold values from -6 to 6
- right_modes: bfloat16 [32, 2, 12, 4096], P('mode', None, None, 'space'), may hold values from -6 to 6
- momenta: int32 [16, 3], replicated, may hold values from -2 to 2
- coords: int32 [3, 4096], P(None, 'space'), may hold values from 0 to 95
Outputs:
- meson_field: float32 [4096, 16, 2, 32], P(('mode', 'space'))
All inputs are finite; a program needn't handle non-finite values.
Results may differ from a plain program's by a relative error of at most 0.0028.
Values may be sent and summed in bfloat16 or wider, within the bound.
No kernel may reach another device: no remote copies, remote signals or barrier semaphores. Data moves between devices by JAX's collectives and lax.ppermute only.
A program may use at most 64 MiB of HBM per device.

v0:
```python
import math

import jax
import jax.numpy as jnp
from jax import lax
from jax.sharding import PartitionSpec as P

EXTENT = 96


def phase_tables(momenta, coords):
    phase_turns = jnp.mod(jnp.sum(momenta[:, :, None] * coords[None, :, :], axis=1), EXTENT)
    angles = phase_turns.astype(jnp.float32) * (2.0 * math.pi / EXTENT)
    return (jnp.cos(angles), jnp.sin(angles))


def phased_block(right_piece, cosines, sines):
    piece_rows = right_piece.shape[0]
    real_part = right_piece[:, 0].astype(jnp.float32)[None]
    imag_part = right_piece[:, 1].astype(jnp.float32)[None]
    cos_wide = cosines[:, None, None, :]
    sin_wide = sines[:, None, None, :]
    turned_re = (cos_wide * real_part + sin_wide * imag_part).astype(jnp.bfloat16)
    turned_im = (cos_wide * imag_part - sin_wide * real_part).astype(jnp.bfloat16)
    upper_half = jnp.stack([turned_re, turned_im], axis=2)
    lower_half = jnp.stack([turned_im, -turned_re], axis=2)
    stacked = jnp.stack([upper_half, lower_half], axis=1)
    return stacked.reshape(cosines.shape[0] * 2 * piece_rows, -1)


def tile_terms(left_mat, right_piece, cosines, sines):
    stacked = phased_block(right_piece, cosines, sines)
    product = lax.dot_general(
        stacked, left_mat, (((1,), (0,)), ((), ())), preferred_element_type=jnp.float32
    )
    return product.reshape(cosines.shape[0], 2, right_piece.shape[0], left_mat.shape[1])


def body(left_modes, right_modes, momenta, coords):
    cosines, sines = phase_tables(momenta, coords)
    left_mat = left_modes.reshape(-1, left_modes.shape[-1])
    norm_scale = 1.0 / math.sqrt(12 * coords.shape[1] * lax.axis_size("space"))
    partial_value = tile_terms(
        left_mat, lax.all_gather(right_modes, "mode", axis=0, tiled=True), cosines, sines
    )
    owned = lax.psum_scatter(partial_value, "space", scatter_dimension=3, tiled=True)
    summed = jnp.transpose(owned, (3, 0, 1, 2))
    return summed * norm_scale


def solution(mesh):
    in_specs = (
        P(None, None, "space", "mode"),
        P("mode", None, None, "space"),
        P(),
        P(None, "space"),
    )
    out_specs = P(("mode", "space"), None, None, None)
    return jax.shard_map(body, mesh=mesh, in_specs=in_specs, out_specs=out_specs, check_vma=False)
```

profile of v0, /device:TPU:6, one launch (start us, length us, event | category | flops | bytes accessed | tf_op | source)
XLA Modules:
  0.0 231.0 jit_solution(12125679252218744204)
XLA Ops:
  6.5 0.0 copy-start
  6.5 0.0 reduce-scatter.2.cloned.1.call-start
  6.5 0.9 multiply_reduce_fusion
  7.4 0.1 fusion.13
  7.5 27.4 %all_gather.3 = bf16[32,2,12,128]{3,1,2,0:T(2,128)(2,1)S(1)} all-gather(bf16[2,2,12,128]{3,1,2,0:T(2,128)(2,1)} %param.5), channel_id=1, replica_groups=mesh['space'=32,'mode'=16] {'mode'}, dimensions={0}, use_global_device_ids=true | all-gather | bytes 208896 | tf_op jit(solution)/shard_map/all_gather | solution.py:44
  34.9 0.3 fusion.16
  35.2 0.5 fusion.15
  35.7 0.8 add_convert_fusion
  36.6 0.5 maximum_bitcast_fusion
  37.1 0.0 copy-done
  37.1 8.3 %fusion.4 = f32[16,2,32,256]{2,3,1,0:T(8,128)} fusion(bf16[16,1,32,2,12,128]{5,2,4,3,1,0:T(8,128)(2,1)S(1)} %get-tuple-element.6, bf16[16,1,32,2,12,128]{5,2,4,3,1,0:T(8,128)(2,1)S(1)} %get-tuple-element.5, bf16[2,12,128,256]{3,2,1,0:T(8,128)(2,1)S(1)} %copy-done), kind=kOutput, calls=%fused_computation.8 | convolution fusion | flops 1613758464 | bytes 8912896 | tf_op jit(solution)/shard_map/dot_general | solution.py:33
  45.3 0.0 reduce-scatter.2.cloned.1.call-update
  45.4 177.2 %reduce-scatter.2.cloned.1.call-done = f32[16,2,32,8]{2,3,1,0:T(8,128)} async-done(((f32[16,2,32,256]{2,3,1,0:T(8,128)}), f32[16,2,32,8]{2,3,1,0:T(8,128)}) %reduce-scatter.2.cloned.1.call-update) | async-done | bytes 32784 | tf_op jit(solution)/shard_map/reduce_scatter | solution.py:46
  222.6 0.9 multiply_bitcast_fusion
  223.5 0.7 copy.26
  (1 shorter events, 0.0 us)
Async XLA Ops:
  6.5 30.5 %copy-start = (bf16[2,12,128,256]{3,2,1,0:T(8,128)(2,1)S(1)}, bf16[2,12,128,256]{3,2,1,0:T(8,128)(2,1)}, u32[]{:S(2)}) copy-start(bf16[2,12,128,256]{3,2,1,0:T(8,128)(2,1)} %param.4) | copy-start | bytes 4718596
  6.5 216.0 %reduce-scatter.2.cloned.1.call-start = ((), (), s32[]{:S(2)}) async-start(), calls=%async_computation.1 | async-start | bytes 4325376 | tf_op jit(solution)/shard_map/reduce_scatter | solution.py:46
Sparse Core Ops, SparseCore 0:
  45.5 177.0 reduce-scatter.1
where the time goes:
time: 231 us
  waiting for transfers between devices  177 us (77%)
  blocking collectives  27.4 us (12%)
  between operations  13.4 us (6%)
  matrix products  8.26 us (4%)
  other arithmetic  3.73 us (2%)
    reduce_scatter x1, waiting for transfers between devices, body(): lax.psum_scatter(partial_value, 'space', scatter_dimension=3, tiled=True)  177 us
    all_gather x1, blocking collectives, body(): lax.all_gather(right_modes, 'mode', axis=0, tiled=True)  27.4 us
    dot_general x1, matrix products, tile_terms(): lax.dot_general(stacked, left_mat, (((1,), (0,)), ((), ())), preferred_el...  8.26 us
  transfers between devices with their start and end apart: 1, of which 1 were waited for; matrix products, arithmetic and copies ran while one was open for 0% of the time, Pallas kernels for 0%

commit v1 on v0

v1 whole, which is shorter than its diff:
```python
import functools
import math

import jax
import jax.numpy as jnp
from jax import lax
from jax.experimental import pallas as pl
from jax.experimental.pallas import tpu as pltpu
from jax.sharding import PartitionSpec as P

EXTENT = 96


def phase_tables(momenta, coords):
    phase_turns = jnp.mod(jnp.sum(momenta[:, :, None] * coords[None, :, :], axis=1), EXTENT)
    angles = phase_turns.astype(jnp.float32) * (2.0 * math.pi / EXTENT)
    return (jnp.cos(angles), jnp.sin(angles))


def partial_kernel(left_ref, right_ref, cos_ref, sin_ref, out_ref):
    rows, depth = right_ref.shape
    modes = rows // 2
    comps = depth // cos_ref.shape[1]
    row = lax.broadcasted_iota(jnp.int32, (rows, rows), 0)
    col = lax.broadcasted_iota(jnp.int32, (rows, rows), 1)
    mode, part = row % modes, row // modes
    pick = jnp.where(col == 2 * mode + part, 1.0, 0.0).astype(jnp.bfloat16)
    sign = jnp.where(part == 0, 1.0, -1.0)
    swap = jnp.where(col == 2 * mode + 1 - part, sign, 0.0).astype(jnp.bfloat16)
    plain = jnp.dot(pick, right_ref[...], preferred_element_type=jnp.float32)
    other = jnp.dot(swap, right_ref[...], preferred_element_type=jnp.float32)
    for p in range(cos_ref.shape[0]):
        cos_row = jnp.concatenate([cos_ref[p : p + 1, :]] * comps, axis=1)
        sin_row = jnp.concatenate([sin_ref[p : p + 1, :]] * comps, axis=1)
        first = (cos_row * plain + sin_row * other).astype(jnp.bfloat16)
        second = (cos_row * other - sin_row * plain).astype(jnp.bfloat16)
        tile = jnp.dot(first, left_ref[0], preferred_element_type=jnp.float32)
        tile += jnp.dot(second, left_ref[1], preferred_element_type=jnp.float32)
        out_ref[:, p * rows : (p + 1) * rows] = tile.T.astype(out_ref.dtype)


def partial_tile(left, right, cosines, sines):
    rows, depth = right.shape
    columns = left.shape[2]
    return pl.pallas_call(
        partial_kernel,
        out_shape=jax.ShapeDtypeStruct((columns, cosines.shape[0] * rows), jnp.bfloat16),
        in_specs=[pl.BlockSpec(memory_space=pltpu.VMEM)] * 4,
        out_specs=pl.BlockSpec(memory_space=pltpu.VMEM),
        compiler_params=pltpu.CompilerParams(vmem_limit_bytes=40 << 20),
    )(left, right, cosines, sines)


def body(left_modes, right_modes, momenta, coords):
    cosines, sines = phase_tables(momenta, coords)
    space, mode = lax.axis_size("space"), lax.axis_size("mode")
    held, _, comps, sites = right_modes.shape
    columns = left_modes.shape[-1]
    momentum_count = momenta.shape[0]
    norm_scale = 1.0 / math.sqrt(comps * sites * space)
    own = right_modes.reshape(1, 2 * held, comps * sites)
    right = lax.all_to_all(jnp.broadcast_to(own, (mode,) + own.shape[1:]), "mode", 0, 0, tiled=True)
    right = right.reshape(mode * 2 * held, comps * sites)
    left = left_modes.reshape(2, comps * sites, columns)
    tile = partial_tile(left, right, cosines, sines)
    pieces = tile.reshape(space, columns // space, tile.shape[1])
    owned = lax.all_to_all(pieces, "space", 0, 0, tiled=True)
    summed = jnp.sum(owned.astype(jnp.float32), axis=0) * norm_scale
    return summed.reshape(columns // space, momentum_count, 2, mode * held)


def solution(mesh):
    in_specs = (
        P(None, None, "space", "mode"),
        P("mode", None, None, "space"),
        P(),
        P(None, "space"),
    )
    out_specs = P(("mode", "space"), None, None, None)
    return jax.shard_map(body, mesh=mesh, in_specs=in_specs, out_specs=out_specs, check_vma=False)
```

time: 231 us -> 62.6 us (0.27)
  the two profiles are of different devices: /device:TPU:6 before, /device:TPU:8 now
where the time goes in v1:
time: 62.6 us; the launch traced here: 62.3 us
  blocking collectives  29.3 us (47%)
  starting transfers between devices  12.8 us (20%)
  waiting for transfers between devices  10.5 us (17%)
  Pallas kernels  4.97 us (8%)
  local copies, waits for them, and re-layouts  3.71 us (6%)
  other arithmetic  0.93 us (1%)
    all_to_all x1, blocking collectives, body(): owned = lax.all_to_all(pieces, 'space', 0, 0, tiled=True)  29.3 us
    all_to_all x1, starting transfers between devices, body(): lax.all_to_all(jnp.broadcast_to(own, (mode,) + own.shape[1:]), 'mode', 0,...  12.8 us
    all_to_all x1, waiting for transfers between devices, body(): lax.all_to_all(jnp.broadcast_to(own, (mode,) + own.shape[1:]), 'mode', 0,...  10.5 us
    pallas_call x1, Pallas kernels, partial_tile(): pl.pallas_call(partial_kernel, out_shape=jax.ShapeDtypeStruct((columns, c...  4.97 us
    unnamed x4, local copies, waits for them, and re-layouts  2.12 us
  transfers between devices with their start and end apart: 1, of which 1 were waited for; matrix products, arithmetic and copies ran while one was open for 1% of the time, Pallas kernels for 0%

profile of v1, /device:TPU:8, one launch (start us, length us, event | category | flops | bytes accessed | tf_op | source)
XLA Modules:
  0.0 62.3 jit_solution(8544013531907783706)
XLA Ops:
  0.0 0.7 %copy.8 = bf16[2,2,12,128]{3,2,1,0:T(8,128)(2,1)S(1)} copy(bf16[2,2,12,128]{3,1,2,0:T(2,128)(2,1)} %param.5) | data formatting | bytes 24576 | tf_op args[1]
  0.7 0.7 %broadcast_in_dim.10 = bf16[16,4,1536]{2,1,0:T(4,128)(2,1)} broadcast(bf16[4,1536]{1,0:T(4,128)(2,1)S(1)} %bitcast.10), dimensions={1,2} | broadcast | bytes 208896 | tf_op jit(solution)/shard_map/broadcast_in_dim | solution.py:62
  1.4 12.8 %all-to-all-start = ((bf16[16,4,1536]{2,1,0:T(4,128)(2,1)}), bf16[16,4,1536]{2,1,0:T(4,128)(2,1)S(1)}, u32[]{:S(2)}, u32[]{:S(2)}) async-start(bf16[16,4,1536]{2,1,0:T(4,128)(2,1)} %broadcast_in_dim.10), calls=%async_computation | async-start | bytes 393216 | tf_op jit(solution)/shard_map/all_to_all | solution.py:62
  14.3 0.8 %multiply_reduce_fusion = s32[16,128]{1,0:T(8,128)S(1)} fusion(s32[3,128]{1,0:T(4,128)} %param.7, s32[16,3]{0,1:T(4,128)} %param.6), kind=kLoop, calls=%fused_computation.1 | loop fusion | flops 10240 | bytes 9920 | tf_op jit(solution)/shard_map/reduce_sum | solution.py:15
  15.1 0.1 fusion.2
  15.1 10.5 %all-to-all-done = bf16[16,4,1536]{2,1,0:T(4,128)(2,1)S(1)} async-done(((bf16[16,4,1536]{2,1,0:T(4,128)(2,1)}), bf16[16,4,1536]{2,1,0:T(4,128)(2,1)S(1)}, u32[]{:S(2)}, u32[]{:S(2)}) %all-to-all-start) | async-done | bytes 196640 | tf_op jit(solution)/shard_map/all_to_all | solution.py:62
  25.7 0.1 reshape.18.right_ref
  25.7 0.0 copy-start
  25.7 1.4 %copy-done = bf16[2,12,128,256]{3,2,1,0:T(8,128)(2,1)S(1)} copy-done((bf16[2,12,128,256]{3,2,1,0:T(8,128)(2,1)S(1)}, bf16[2,12,128,256]{3,2,1,0:T(8,128)(2,1)}, u32[]{:S(2)}) %copy-start) | copy-done | bytes 1572888
  27.1 5.0 %shard_map.46 = bf16[256,1024]{1,0:T(8,128)(2,1)S(1)} custom-call(bf16[2,1536,256]{2,1,0:T(8,128)(2,1)S(1)} %bitcast.8, bf16[64,1536]{1,0:T(8,128)(2,1)S(1)} %reshape.18.right_ref, f32[16,128]{1,0:T(8,128)S(1)} %get-tuple-element.6.cos_ref, f32[16,128]{1,0:T(8,128)S(1)} %get-tuple-element.5.sin_ref), custom_call_target="tpu_custom_call" | custom-call | tf_op jit(solution)/shard_map/pallas_call | solution.py:45
  32.1 29.3 %all_to_all.10 = bf16[32,8,1024]{2,1,0:T(8,128)(2,1)S(1)} all-to-all(bf16[32,8,1024]{2,1,0:T(8,128)(2,1)S(1)} %bitcast.7), channel_id=1, replica_groups=mesh['space'=32,'mode'=16] {'space'}, dimensions={0} | all-to-all | bytes 1048576 | tf_op jit(solution)/shard_map/all_to_all | solution.py:67
  61.4 0.1 convert_reduce_fusion
  61.5 0.8 %mul.36 = f32[8,16,2,32]{3,2,1,0:T(2,128)} reshape(f32[8,1024]{1,0:T(8,128)S(1)} %broadcast_multiply_fusion) | data formatting | bytes 65536 | tf_op jit(solution)/shard_map/mul | solution.py:68
  (2 shorter events, 0.0 us)
Async XLA Ops:
  1.4 24.2 %all-to-all-start = ((bf16[16,4,1536]{2,1,0:T(4,128)(2,1)}), bf16[16,4,1536]{2,1,0:T(4,128)(2,1)S(1)}, u32[]{:S(2)}, u32[]{:S(2)}) async-start(bf16[16,4,1536]{2,1,0:T(4,128)(2,1)} %broadcast_in_dim.10), calls=%async_computation | async-start | bytes 393216 | tf_op jit(solution)/shard_map/all_to_all | solution.py:62
  25.7 1.4 %copy-start = (bf16[2,12,128,256]{3,2,1,0:T(8,128)(2,1)S(1)}, bf16[2,12,128,256]{3,2,1,0:T(8,128)(2,1)}, u32[]{:S(2)}) copy-start(bf16[2,12,128,256]{3,2,1,0:T(8,128)(2,1)} %param.4) | copy-start | bytes 4718596

commit v2 on v1

v2 whole, which is shorter than its diff:
```python
import math

import jax
import jax.numpy as jnp
from jax import lax
from jax.experimental import pallas as pl
from jax.experimental.pallas import tpu as pltpu
from jax.sharding import PartitionSpec as P

EXTENT = 96
GROUP = 4
NT = (((1,), (1,)), ((), ()))


def phase_tables(momenta, coords):
    phase_turns = jnp.mod(jnp.sum(momenta[:, :, None] * coords[None, :, :], axis=1), EXTENT)
    angles = phase_turns.astype(jnp.float32) * (2.0 * math.pi / EXTENT)
    return (jnp.cos(angles), jnp.sin(angles))


def turn_kernel(left_ref, out_ref):
    columns = left_ref.shape[2]
    for part in range(2):
        out_ref[part * columns : (part + 1) * columns, :] = left_ref[part].T


def turned_left(left):
    _, depth, columns = left.shape
    return pl.pallas_call(
        turn_kernel,
        out_shape=jax.ShapeDtypeStruct((2 * columns, depth), left.dtype),
        in_specs=[pl.BlockSpec(memory_space=pltpu.VMEM)],
        out_specs=pl.BlockSpec(memory_space=pltpu.VMEM),
        cost_estimate=pl.CostEstimate(flops=0, transcendentals=0, bytes_accessed=4 * left.size),
        compiler_params=pltpu.CompilerParams(vmem_limit_bytes=16 << 20),
        name="turn_left",
    )(left)


def partial_kernel(left_ref, right_ref, cos_ref, sin_ref, out_ref, plain_ref, rows_ref):
    momenta, sites = cos_ref.shape
    depth = left_ref.shape[1]
    comps = depth // sites
    modes = right_ref.shape[0] // (2 * comps)
    columns = out_ref.shape[0]
    half = GROUP * modes
    plain_ref[...] = right_ref[...].astype(jnp.float32)
    for q in range(momenta // GROUP):
        slot = q % 2
        for c in range(comps):
            real = plain_ref[pl.ds(2 * c, modes, stride=2 * comps), :]
            imag = plain_ref[pl.ds(2 * c + 1, modes, stride=2 * comps), :]
            lanes = slice(c * sites, (c + 1) * sites)
            for k in range(GROUP):
                p = q * GROUP + k
                cos_row, sin_row = cos_ref[p : p + 1, :], sin_ref[p : p + 1, :]
                turned_re = (cos_row * real + sin_row * imag).astype(jnp.bfloat16)
                turned_im = (cos_row * imag - sin_row * real).astype(jnp.bfloat16)
                rows_ref[slot, k * modes : (k + 1) * modes, lanes] = turned_re
                rows_ref[slot, half + k * modes : half + (k + 1) * modes, lanes] = turned_im
        both = lax.dot_general(left_ref[...], rows_ref[slot], NT, preferred_element_type=jnp.float32)
        upper, lower = both[:columns], both[columns:]
        base = q * 2 * half
        out_ref[:, base : base + half] = (upper[:, :half] + lower[:, half:]).astype(out_ref.dtype)
        out_ref[:, base + half : base + 2 * half] = (upper[:, half:] - lower[:, :half]).astype(out_ref.dtype)


def partial_tile(left, right, cosines, sines):
    rows, sites = right.shape
    columns, depth = left.shape[0] // 2, left.shape[1]
    modes = rows * sites // (2 * depth)
    momenta = cosines.shape[0]
    return pl.pallas_call(
        partial_kernel,
        out_shape=jax.ShapeDtypeStruct((columns, momenta * 2 * modes), jnp.bfloat16),
        in_specs=[pl.BlockSpec(memory_space=pltpu.VMEM)] * 4,
        out_specs=pl.BlockSpec(memory_space=pltpu.VMEM),
        scratch_shapes=[
            pltpu.VMEM((rows, sites), jnp.float32),
            pltpu.VMEM((2, 2 * GROUP * modes, depth), jnp.bfloat16),
        ],
        compiler_params=pltpu.CompilerParams(vmem_limit_bytes=32 << 20),
        name="partial_tile",
    )(left, right, cosines, sines)


def sum_kernel(scale, pieces_ref, out_ref):
    _, momenta, parts, modes = out_ref.shape
    total = jnp.sum(pieces_ref[...].astype(jnp.float32), axis=0) * scale
    for p in range(momenta):
        for part in range(parts):
            group, k = divmod(p, GROUP)
            start = ((group * parts + part) * GROUP + k) * modes
            out_ref[:, p, part, :] = total[:, start : start + modes]


def owned_sum(pieces, momenta, scale):
    _, rows, width = pieces.shape
    return pl.pallas_call(
        lambda a, b: sum_kernel(scale, a, b),
        out_shape=jax.ShapeDtypeStruct((rows, momenta, 2, width // (2 * momenta)), jnp.float32),
        in_specs=[pl.BlockSpec(memory_space=pltpu.VMEM)],
        out_specs=pl.BlockSpec(memory_space=pltpu.VMEM),
        compiler_params=pltpu.CompilerParams(vmem_limit_bytes=8 << 20),
        name="owned_sum",
    )(pieces)


def body(left_modes, right_modes, momenta, coords):
    cosines, sines = phase_tables(momenta, coords)
    space, mode = lax.axis_size("space"), lax.axis_size("mode")
    held, _, comps, sites = right_modes.shape
    columns = left_modes.shape[-1]
    norm_scale = 1.0 / math.sqrt(comps * sites * space)
    own = right_modes.transpose(0, 2, 1, 3).reshape(1, held * comps * 2, sites)
    right = lax.all_to_all(jnp.broadcast_to(own, (mode,) + own.shape[1:]), "mode", 0, 0, tiled=True)
    left = turned_left(left_modes.reshape(2, comps * sites, columns))
    tile = partial_tile(left, right.reshape(-1, sites), cosines, sines)
    pieces = tile.reshape(space, columns // space, tile.shape[1])
    owned = lax.all_to_all(pieces, "space", 0, 0, tiled=True)
    return owned_sum(owned, momenta.shape[0], norm_scale)


def solution(mesh):
    in_specs = (
        P(None, None, "space", "mode"),
        P("mode", None, None, "space"),
        P(),
        P(None, "space"),
    )
    out_specs = P(("mode", "space"), None, None, None)
    return jax.shard_map(body, mesh=mesh, in_specs=in_specs, out_specs=out_specs, check_vma=False)
```

time: 62.6 us -> 58.6 us (0.936)
  waiting for transfers between devices: 10.5 us -> 9.1 us
  Pallas kernels: 4.97 us -> 3.77 us
  other arithmetic: 0.93 us -> 0.14 us
  local copies, waits for them, and re-layouts: 3.71 us -> 3.04 us
    all_to_all x1, waiting for transfers between devices: 10.5 us -> 9.1 us  [body(): lax.all_to_all(jnp.broadcast_to(own, (mode,) + own.shape[1:]), 'mode', 0,...]
    pallas_call x1 -> x3, Pallas kernels: 4.97 us -> 3.77 us  [the longest x1 2.35 us: partial_tile(): pl.pallas_call(partial_kernel, out_shape=jax.ShapeDtypeStruct((columns, m...]
    mul x1 -> x0, local copies, waits for them, and re-layouts: 0.81 us -> none  [body(): summed = jnp.sum(owned.astype(jnp.float32), axis=0) * norm_scale]
    reduce_sum x1, other arithmetic: 0.77 us -> 0.07 us  [phase_tables(): jnp.sum(momenta[:, :, None] * coords[None, :, :], axis=1)]
    broadcast_in_dim x1, local copies, waits for them, and re-layouts: 0.72 us -> 1.4 us  [body(): jnp.broadcast_to(own, (mode,) + own.shape[1:])]
    unnamed x4 -> x6, local copies, waits for them, and re-layouts: 2.12 us -> 1.64 us
  transfers between devices with their start and end apart: 1 -> 1, of which waited for: 1 -> 1; matrix products, arithmetic and copies ran while one was open for 1% -> 0% of each run, Pallas kernels for 0% -> 1%
where the time goes in v2:
time: 58.6 us; the launch traced here: 58.2 us
  blocking collectives  29.3 us (50%)
  starting transfers between devices  12.8 us (22%)
  waiting for transfers between devices  9.1 us (16%)
  Pallas kernels  3.77 us (6%)
  local copies, waits for them, and re-layouts  3.04 us (5%)
    all_to_all x1, blocking collectives, body(): owned = lax.all_to_all(pieces, 'space', 0, 0, tiled=True)  29.3 us
    all_to_all x1, starting transfers between devices, body(): lax.all_to_all(jnp.broadcast_to(own, (mode,) + own.shape[1:]), 'mode', 0,...  12.8 us
    all_to_all x1, waiting for transfers between devices, body(): lax.all_to_all(jnp.broadcast_to(own, (mode,) + own.shape[1:]), 'mode', 0,...  9.1 us
    pallas_call x1, Pallas kernels, partial_tile(): pl.pallas_call(partial_kernel, out_shape=jax.ShapeDtypeStruct((columns, m...  2.35 us
    unnamed x6, local copies, waits for them, and re-layouts  1.64 us
    broadcast_in_dim x1, local copies, waits for them, and re-layouts, body(): jnp.broadcast_to(own, (mode,) + own.shape[1:])  1.4 us
  transfers between devices with their start and end apart: 1, of which 1 were waited for; matrix products, arithmetic and copies ran while one was open for 0% of the time, Pallas kernels for 1%

profile of v2, /device:TPU:8, one launch (start us, length us, event | category | flops | bytes accessed | tf_op | source)
XLA Modules:
  0.0 58.2 jit_solution(3155410433504629962)
XLA Ops:
  0.0 1.4 %broadcast_in_dim.10 = bf16[16,48,128]{2,1,0:T(8,128)(2,1)} broadcast(bf16[48,128]{1,0:T(8,128)(2,1)} %bitcast.9), dimensions={1,2} | broadcast | bytes 208896 | tf_op jit(solution)/shard_map/broadcast_in_dim | solution.py:116
  1.4 12.8 %all-to-all-start = ((bf16[16,48,128]{2,1,0:T(8,128)(2,1)}), bf16[16,48,128]{2,1,0:T(8,128)(2,1)S(1)}, u32[]{:S(2)}, u32[]{:S(2)}) async-start(bf16[16,48,128]{2,1,0:T(8,128)(2,1)} %broadcast_in_dim.10), calls=%async_computation | async-start | bytes 393216 | tf_op jit(solution)/shard_map/all_to_all | solution.py:116
  14.3 0.0 copy-start
  14.3 1.4 %copy-done = bf16[2,12,128,256]{3,2,1,0:T(8,128)(2,1)S(1)} copy-done((bf16[2,12,128,256]{3,2,1,0:T(8,128)(2,1)S(1)}, bf16[2,12,128,256]{3,2,1,0:T(8,128)(2,1)}, u32[]{:S(2)}) %copy-start) | copy-done | bytes 1572888
  15.7 0.0 copy-start.1
  15.7 0.0 copy-start.2
  15.7 0.5 turn_left.1.left_ref
  16.1 0.2 copy-done.1
  16.4 0.0 copy-done.2
  16.4 0.1 multiply_reduce_fusion
  16.4 0.1 fusion.2
  16.5 9.1 %all-to-all-done = bf16[16,48,128]{2,1,0:T(8,128)(2,1)S(1)} async-done(((bf16[16,48,128]{2,1,0:T(8,128)(2,1)}), bf16[16,48,128]{2,1,0:T(8,128)(2,1)S(1)}, u32[]{:S(2)}, u32[]{:S(2)}) %all-to-all-start) | async-done | bytes 196640 | tf_op jit(solution)/shard_map/all_to_all | solution.py:116
  25.6 2.4 %partial_tile.1 = bf16[256,1024]{1,0:T(8,128)(2,1)S(1)} custom-call(bf16[512,1536]{1,0:T(8,128)(2,1)S(1)} %turn_left.1.left_ref, bf16[768,128]{1,0:T(8,128)(2,1)S(1)} %bitcast.8, f32[16,128]{1,0:T(8,128)S(1)} %get-tuple-element.6.cos_ref, f32[16,128]{1,0:T(8,128)S(1)} %get-tuple-element.5.sin_ref), custom_call_target="tpu_custom_call" | custom-call | tf_op jit(solution)/shard_map/partial_tile/pallas_call | solution.py:73
  28.0 29.3 %all_to_all.10.a = bf16[32,8,1024]{2,1,0:T(8,128)(2,1)S(1)} all-to-all(bf16[32,8,1024]{2,1,0:T(8,128)(2,1)S(1)} %bitcast.6), channel_id=1, replica_groups=mesh['space'=32,'mode'=16] {'space'}, dimensions={0} | all-to-all | bytes 1048576 | tf_op jit(solution)/shard_map/all_to_all | solution.py:120
  57.3 1.0 %owned_sum.1 = f32[8,16,2,32]{3,2,1,0:T(2,128)} custom-call(bf16[32,8,1024]{2,1,0:T(8,128)(2,1)S(1)} %all_to_all.10.a), custom_call_target="tpu_custom_call" | custom-call | tf_op jit(solution)/shard_map/owned_sum/pallas_call | solution.py:99
Async XLA Ops:
  1.4 24.2 %all-to-all-start = ((bf16[16,48,128]{2,1,0:T(8,128)(2,1)}), bf16[16,48,128]{2,1,0:T(8,128)(2,1)S(1)}, u32[]{:S(2)}, u32[]{:S(2)}) async-start(bf16[16,48,128]{2,1,0:T(8,128)(2,1)} %broadcast_in_dim.10), calls=%async_computation | async-start | bytes 393216 | tf_op jit(solution)/shard_map/all_to_all | solution.py:116
  14.3 1.4 %copy-start = (bf16[2,12,128,256]{3,2,1,0:T(8,128)(2,1)S(1)}, bf16[2,12,128,256]{3,2,1,0:T(8,128)(2,1)}, u32[]{:S(2)}) copy-start(bf16[2,12,128,256]{3,2,1,0:T(8,128)(2,1)} %param.4) | copy-start | bytes 4718596
  15.7 0.7 %copy-start.1 = (s32[3,128]{1,0:T(4,128)S(1)}, s32[3,128]{1,0:T(4,128)}, u32[]{:S(2)}) copy-start(s32[3,128]{1,0:T(4,128)} %param.7) | copy-start | bytes 4612
  15.7 0.7 %copy-start.2 = (s32[16,3]{0,1:T(4,128)S(1)}, s32[16,3]{0,1:T(4,128)}, u32[]{:S(2)}) copy-start(s32[16,3]{0,1:T(4,128)} %param.6) | copy-start | bytes 580

commit v3 on v2

--- a/solution.py
+++ b/solution.py
@@ -1,3 +1,4 @@
+import functools
 import math
 
 import jax
@@ -9,6 +10,8 @@
 
 EXTENT = 96
 GROUP = 4
+MODE_FIRST = 15
+SPACE_FIRST = 30
 NT = (((1,), (1,)), ((), ()))
 
 
@@ -18,16 +21,23 @@
     return (jnp.cos(angles), jnp.sin(angles))
 
 
-def turn_kernel(left_ref, out_ref):
+def led_by(first, count):
+    return [(first + k) % count for k in range(count)]
+
+
+def turn_kernel(skip, left_ref, out_ref):
     columns = left_ref.shape[2]
     for part in range(2):
-        out_ref[part * columns : (part + 1) * columns, :] = left_ref[part].T
+        turned = left_ref[part].T
+        base = part * columns
+        out_ref[base : base + columns - skip, :] = turned[skip:, :]
+        out_ref[base + columns - skip : base + columns, :] = turned[:skip, :]
 
 
-def turned_left(left):
+def turned_left(left, skip):
     _, depth, columns = left.shape
     return pl.pallas_call(
-        turn_kernel,
+        functools.partial(turn_kernel, skip),
         out_shape=jax.ShapeDtypeStruct((2 * columns, depth), left.dtype),
         in_specs=[pl.BlockSpec(memory_space=pltpu.VMEM)],
         out_specs=pl.BlockSpec(memory_space=pltpu.VMEM),
@@ -37,14 +47,16 @@
     )(left)
 
 
-def partial_kernel(left_ref, right_ref, cos_ref, sin_ref, out_ref, plain_ref, rows_ref):
+def partial_kernel(first, members, left_ref, right_ref, cos_ref, sin_ref, out_ref, plain_ref, rows_ref):
     momenta, sites = cos_ref.shape
     depth = left_ref.shape[1]
     comps = depth // sites
     modes = right_ref.shape[0] // (2 * comps)
     columns = out_ref.shape[0]
     half = GROUP * modes
-    plain_ref[...] = right_ref[...].astype(jnp.float32)
+    skip = first * right_ref.shape[0] // members
+    plain_ref[skip:, :] = right_ref[: right_ref.shape[0] - skip, :].astype(jnp.float32)
+    plain_ref[:skip, :] = right_ref[right_ref.shape[0] - skip :, :].astype(jnp.float32)
     for q in range(momenta // GROUP):
         slot = q % 2
         for c in range(comps):
@@ -65,13 +77,13 @@
         out_ref[:, base + half : base + 2 * half] = (upper[:, half:] - lower[:, :half]).astype(out_ref.dtype)
 
 
-def partial_tile(left, right, cosines, sines):
+def partial_tile(left, right, cosines, sines, first, members):
     rows, sites = right.shape
     columns, depth = left.shape[0] // 2, left.shape[1]
     modes = rows * sites // (2 * depth)
     momenta = cosines.shape[0]
     return pl.pallas_call(
-        partial_kernel,
+        functools.partial(partial_kernel, first, members),
         out_shape=jax.ShapeDtypeStruct((columns, momenta * 2 * modes), jnp.bfloat16),
         in_specs=[pl.BlockSpec(memory_space=pltpu.VMEM)] * 4,
         out_specs=pl.BlockSpec(memory_space=pltpu.VMEM),
@@ -112,12 +124,18 @@
     held, _, comps, sites = right_modes.shape
     columns = left_modes.shape[-1]
     norm_scale = 1.0 / math.sqrt(comps * sites * space)
-    own = right_modes.transpose(0, 2, 1, 3).reshape(1, held * comps * 2, sites)
-    right = lax.all_to_all(jnp.broadcast_to(own, (mode,) + own.shape[1:]), "mode", 0, 0, tiled=True)
-    left = turned_left(left_modes.reshape(2, comps * sites, columns))
-    tile = partial_tile(left, right.reshape(-1, sites), cosines, sines)
-    pieces = tile.reshape(space, columns // space, tile.shape[1])
-    owned = lax.all_to_all(pieces, "space", 0, 0, tiled=True)
+    own = right_modes.transpose(0, 2, 1, 3).reshape(held * comps * 2, sites)
+    mode_first, space_first = MODE_FIRST % mode, SPACE_FIRST % space
+    right = lax.all_to_all(
+        jnp.broadcast_to(own[None], (mode,) + own.shape), "mode", 0, 0, axis_index_groups=[led_by(mode_first, mode)], tiled=True
+    )
+    rows = columns // space
+    left = turned_left(left_modes.reshape(2, comps * sites, columns), space_first * rows)
+    tile = partial_tile(left, right.reshape(-1, sites), cosines, sines, mode_first, mode)
+    pieces = tile.reshape(space, rows, tile.shape[1])
+    owned = lax.all_to_all(
+        pieces, "space", 0, 0, axis_index_groups=[led_by(space_first, space)], tiled=True
+    )
     return owned_sum(owned, momenta.shape[0], norm_scale)
 
 

time: 58.6 us -> 48.8 us (0.83)
  the two profiles are of different devices: /device:TPU:8 before, /device:TPU:14 now
where the time goes in v3:
time: 48.8 us; the launch traced here: 48.5 us
  blocking collectives  26 us (53%)
  starting transfers between devices  11.8 us (24%)
  Pallas kernels  3.78 us (8%)
  waiting for transfers between devices  3.7 us (8%)
  local copies, waits for them, and re-layouts  3.04 us (6%)
    all_to_all x1, blocking collectives, body(): lax.all_to_all(pieces, 'space', 0, 0, axis_index_groups=[led_by(space_fir...  26 us
    all_to_all x1, starting transfers between devices, body(): lax.all_to_all(jnp.broadcast_to(own[None], (mode,) + own.shape), 'mode',...  11.8 us
    all_to_all x1, waiting for transfers between devices, body(): lax.all_to_all(jnp.broadcast_to(own[None], (mode,) + own.shape), 'mode',...  3.7 us
    pallas_call x1, Pallas kernels, partial_tile(): pl.pallas_call(functools.partial(partial_kernel, first, members), out_sha...  2.36 us
    unnamed x6, local copies, waits for them, and re-layouts  1.64 us
    broadcast_in_dim x1, local copies, waits for them, and re-layouts, body(): jnp.broadcast_to(own[None], (mode,) + own.shape)  1.4 us
  transfers between devices with their start and end apart: 1, of which 1 were waited for; matrix products, arithmetic and copies ran while one was open for 0% of the time, Pallas kernels for 1%

profile of v3, /device:TPU:14, one launch (start us, length us, event | category | flops | bytes accessed | tf_op | source)
XLA Modules:
  0.0 48.5 jit_solution(7857468457560429149)
XLA Ops:
  0.0 1.4 %broadcast_in_dim.10 = bf16[16,48,128]{2,1,0:T(8,128)(2,1)} broadcast(bf16[48,128]{1,0:T(8,128)(2,1)} %bitcast.9), dimensions={1,2} | broadcast | bytes 208896 | tf_op jit(solution)/shard_map/broadcast_in_dim | solution.py:130
  1.4 11.8 %all-to-all-start = ((bf16[16,48,128]{2,1,0:T(8,128)(2,1)}), bf16[16,48,128]{2,1,0:T(8,128)(2,1)S(1)}, u32[]{:S(2)}, u32[]{:S(2)}) async-start(bf16[16,48,128]{2,1,0:T(8,128)(2,1)} %broadcast_in_dim.10), calls=%async_computation | async-start | bytes 393216 | tf_op jit(solution)/shard_map/all_to_all | solution.py:129
  13.2 0.0 copy-start
  13.2 1.4 %copy-done = bf16[2,12,128,256]{3,2,1,0:T(8,128)(2,1)S(1)} copy-done((bf16[2,12,128,256]{3,2,1,0:T(8,128)(2,1)S(1)}, bf16[2,12,128,256]{3,2,1,0:T(8,128)(2,1)}, u32[]{:S(2)}) %copy-start) | copy-done | bytes 1572888
  14.6 0.0 copy-start.1
  14.6 0.0 copy-start.2
  14.6 0.5 turn_left.1.left_ref
  15.1 0.2 copy-done.1
  15.3 0.0 copy-done.2
  15.3 0.1 multiply_reduce_fusion
  15.4 0.1 fusion.2
  15.5 3.7 %all-to-all-done = bf16[16,48,128]{2,1,0:T(8,128)(2,1)S(1)} async-done(((bf16[16,48,128]{2,1,0:T(8,128)(2,1)}), bf16[16,48,128]{2,1,0:T(8,128)(2,1)S(1)}, u32[]{:S(2)}, u32[]{:S(2)}) %all-to-all-start) | async-done | bytes 196640 | tf_op jit(solution)/shard_map/all_to_all | solution.py:129
  19.2 2.4 %partial_tile.1 = bf16[256,1024]{1,0:T(8,128)(2,1)S(1)} custom-call(bf16[512,1536]{1,0:T(8,128)(2,1)S(1)} %turn_left.1.left_ref, bf16[768,128]{1,0:T(8,128)(2,1)S(1)} %bitcast.8, f32[16,128]{1,0:T(8,128)S(1)} %get-tuple-element.6.cos_ref, f32[16,128]{1,0:T(8,128)S(1)} %get-tuple-element.5.sin_ref), custom_call_target="tpu_custom_call" | custom-call | tf_op jit(solution)/shard_map/partial_tile/pallas_call | solution.py:85
  21.5 26.0 %all_to_all.10.a = bf16[32,8,1024]{2,1,0:T(8,128)(2,1)S(1)} all-to-all(bf16[32,8,1024]{2,1,0:T(8,128)(2,1)S(1)} %bitcast.6), channel_id=1, replica_groups={{480,496,0,16,32,48,64,80,96,112,128,144,160,176,192,208,224,240,256,27..., dimensions={0} | all-to-all | bytes 1048576 | tf_op jit(solution)/shard_map/all_to_all | solution.py:136
  47.5 1.0 %owned_sum.1 = f32[8,16,2,32]{3,2,1,0:T(2,128)} custom-call(bf16[32,8,1024]{2,1,0:T(8,128)(2,1)S(1)} %all_to_all.10.a), custom_call_target="tpu_custom_call" | custom-call | tf_op jit(solution)/shard_map/owned_sum/pallas_call | solution.py:111
Async XLA Ops:
  1.4 17.7 %all-to-all-start = ((bf16[16,48,128]{2,1,0:T(8,128)(2,1)}), bf16[16,48,128]{2,1,0:T(8,128)(2,1)S(1)}, u32[]{:S(2)}, u32[]{:S(2)}) async-start(bf16[16,48,128]{2,1,0:T(8,128)(2,1)} %broadcast_in_dim.10), calls=%async_computation | async-start | bytes 393216 | tf_op jit(solution)/shard_map/all_to_all | solution.py:129
  13.2 1.4 %copy-start = (bf16[2,12,128,256]{3,2,1,0:T(8,128)(2,1)S(1)}, bf16[2,12,128,256]{3,2,1,0:T(8,128)(2,1)}, u32[]{:S(2)}) copy-start(bf16[2,12,128,256]{3,2,1,0:T(8,128)(2,1)} %param.4) | copy-start | bytes 4718596
  14.6 0.7 %copy-start.1 = (s32[3,128]{1,0:T(4,128)S(1)}, s32[3,128]{1,0:T(4,128)}, u32[]{:S(2)}) copy-start(s32[3,128]{1,0:T(4,128)} %param.7) | copy-start | bytes 4612
  14.6 0.7 %copy-start.2 = (s32[16,3]{0,1:T(4,128)S(1)}, s32[16,3]{0,1:T(4,128)}, u32[]{:S(2)}) copy-start(s32[16,3]{0,1:T(4,128)} %param.6) | copy-start | bytes 580

commit v4 on v2

--- a/solution.py
+++ b/solution.py
@@ -1,3 +1,4 @@
+import functools
 import math
 
 import jax
@@ -8,7 +9,16 @@
 from jax.sharding import PartitionSpec as P
 
 EXTENT = 96
-GROUP = 4
+
+
+def counted_from(first, members):
+    start = members.index(first)
+    return members[start:] + members[:start]
+
+
+GROUP = 16
+MODE_ORDER = [8 * h + 2 * x + c for h in (1, 0) for c in (1, 0) for x in (3, 2, 1, 0)]
+SPACE_ORDER = counted_from(22, [4 * y + z for z in range(4) for y in range(8)])
 NT = (((1,), (1,)), ((), ()))
 
 
@@ -18,16 +28,20 @@
     return (jnp.cos(angles), jnp.sin(angles))
 
 
-def turn_kernel(left_ref, out_ref):
+def turn_kernel(order, left_ref, out_ref):
     columns = left_ref.shape[2]
+    rows = columns // len(order)
     for part in range(2):
-        out_ref[part * columns : (part + 1) * columns, :] = left_ref[part].T
+        turned = left_ref[part].T
+        for k, member in enumerate(order):
+            start = part * columns + k * rows
+            out_ref[start : start + rows, :] = turned[member * rows : (member + 1) * rows, :]
 
 
-def turned_left(left):
+def turned_left(left, order):
     _, depth, columns = left.shape
     return pl.pallas_call(
-        turn_kernel,
+        functools.partial(turn_kernel, order),
         out_shape=jax.ShapeDtypeStruct((2 * columns, depth), left.dtype),
         in_specs=[pl.BlockSpec(memory_space=pltpu.VMEM)],
         out_specs=pl.BlockSpec(memory_space=pltpu.VMEM),
@@ -37,14 +51,16 @@
     )(left)
 
 
-def partial_kernel(left_ref, right_ref, cos_ref, sin_ref, out_ref, plain_ref, rows_ref):
+def partial_kernel(order, left_ref, right_ref, cos_ref, sin_ref, out_ref, plain_ref, rows_ref):
     momenta, sites = cos_ref.shape
     depth = left_ref.shape[1]
     comps = depth // sites
     modes = right_ref.shape[0] // (2 * comps)
     columns = out_ref.shape[0]
     half = GROUP * modes
-    plain_ref[...] = right_ref[...].astype(jnp.float32)
+    part = right_ref.shape[0] // len(order)
+    for k, member in enumerate(order):
+        plain_ref[member * part : (member + 1) * part, :] = right_ref[k * part : (k + 1) * part, :].astype(jnp.float32)
     for q in range(momenta // GROUP):
         slot = q % 2
         for c in range(comps):
@@ -65,19 +81,19 @@
         out_ref[:, base + half : base + 2 * half] = (upper[:, half:] - lower[:, :half]).astype(out_ref.dtype)
 
 
-def partial_tile(left, right, cosines, sines):
+def partial_tile(left, right, cosines, sines, order):
     rows, sites = right.shape
     columns, depth = left.shape[0] // 2, left.shape[1]
     modes = rows * sites // (2 * depth)
     momenta = cosines.shape[0]
     return pl.pallas_call(
-        partial_kernel,
+        functools.partial(partial_kernel, order),
         out_shape=jax.ShapeDtypeStruct((columns, momenta * 2 * modes), jnp.bfloat16),
         in_specs=[pl.BlockSpec(memory_space=pltpu.VMEM)] * 4,
         out_specs=pl.BlockSpec(memory_space=pltpu.VMEM),
         scratch_shapes=[
             pltpu.VMEM((rows, sites), jnp.float32),
-            pltpu.VMEM((2, 2 * GROUP * modes, depth), jnp.bfloat16),
+            pltpu.VMEM((min(2, momenta // GROUP), 2 * GROUP * modes, depth), jnp.bfloat16),
         ],
         compiler_params=pltpu.CompilerParams(vmem_limit_bytes=32 << 20),
         name="partial_tile",
@@ -112,12 +128,18 @@
     held, _, comps, sites = right_modes.shape
     columns = left_modes.shape[-1]
     norm_scale = 1.0 / math.sqrt(comps * sites * space)
-    own = right_modes.transpose(0, 2, 1, 3).reshape(1, held * comps * 2, sites)
-    right = lax.all_to_all(jnp.broadcast_to(own, (mode,) + own.shape[1:]), "mode", 0, 0, tiled=True)
-    left = turned_left(left_modes.reshape(2, comps * sites, columns))
-    tile = partial_tile(left, right.reshape(-1, sites), cosines, sines)
-    pieces = tile.reshape(space, columns // space, tile.shape[1])
-    owned = lax.all_to_all(pieces, "space", 0, 0, tiled=True)
+    own = right_modes.transpose(0, 2, 1, 3).reshape(held * comps * 2, sites)
+    order, space_order = MODE_ORDER, SPACE_ORDER
+    right = lax.all_to_all(
+        jnp.broadcast_to(own[None], (mode,) + own.shape), "mode", 0, 0, axis_index_groups=[order], tiled=True
+    )
+    rows = columns // space
+    left = turned_left(left_modes.reshape(2, comps * sites, columns), space_order)
+    tile = partial_tile(left, right.reshape(-1, sites), cosines, sines, order)
+    pieces = tile.reshape(space, rows, tile.shape[1])
+    owned = lax.all_to_all(
+        pieces, "space", 0, 0, axis_index_groups=[space_order], tiled=True
+    )
     return owned_sum(owned, momenta.shape[0], norm_scale)
 
 

time: 58.6 us -> 47.6 us (0.81)
  the two profiles are of different devices: /device:TPU:8 before, /device:TPU:6 now
where the time goes in v4:
time: 47.6 us; the launch traced here: 47 us
  blocking collectives  24.5 us (51%)
  starting transfers between devices  12.2 us (26%)
  waiting for transfers between devices  3.66 us (8%)
  Pallas kernels  3.44 us (7%)
  local copies, waits for them, and re-layouts  3.04 us (6%)
    all_to_all x1, blocking collectives, body(): lax.all_to_all(pieces, 'space', 0, 0, axis_index_groups=[space_order], ti...  24.5 us
    all_to_all x1, starting transfers between devices, body(): lax.all_to_all(jnp.broadcast_to(own[None], (mode,) + own.shape), 'mode',...  12.2 us
    all_to_all x1, waiting for transfers between devices, body(): lax.all_to_all(jnp.broadcast_to(own[None], (mode,) + own.shape), 'mode',...  3.66 us
    pallas_call x1, Pallas kernels, partial_tile(): pl.pallas_call(functools.partial(partial_kernel, order), out_shape=jax.Sh...  2.02 us
    unnamed x6, local copies, waits for them, and re-layouts  1.64 us
    broadcast_in_dim x1, local copies, waits for them, and re-layouts, body(): jnp.broadcast_to(own[None], (mode,) + own.shape)  1.4 us
    pallas_call x1, Pallas kernels, owned_sum(): pl.pallas_call(lambda a, b: sum_kernel(scale, a, b), out_shape=jax.ShapeD...  0.97 us
  transfers between devices with their start and end apart: 1, of which 1 were waited for; matrix products, arithmetic and copies ran while one was open for 0% of the time, Pallas kernels for 1%

profile of v4, /device:TPU:6, one launch (start us, length us, event | category | flops | bytes accessed | tf_op | source)
XLA Modules:
  0.0 47.0 jit_solution(15004023346716421868)
XLA Ops:
  0.0 1.4 %broadcast_in_dim.10 = bf16[16,48,128]{2,1,0:T(8,128)(2,1)} broadcast(bf16[48,128]{1,0:T(8,128)(2,1)} %bitcast.9), dimensions={1,2} | broadcast | bytes 208896 | tf_op jit(solution)/shard_map/broadcast_in_dim | solution.py:134
  1.4 12.2 %all-to-all-start = ((bf16[16,48,128]{2,1,0:T(8,128)(2,1)}), bf16[16,48,128]{2,1,0:T(8,128)(2,1)S(1)}, u32[]{:S(2)}, u32[]{:S(2)}) async-start(bf16[16,48,128]{2,1,0:T(8,128)(2,1)} %broadcast_in_dim.10), calls=%async_computation | async-start | bytes 393216 | tf_op jit(solution)/shard_map/all_to_all | solution.py:133
  13.6 0.0 copy-start
  13.6 1.4 %copy-done = bf16[2,12,128,256]{3,2,1,0:T(8,128)(2,1)S(1)} copy-done((bf16[2,12,128,256]{3,2,1,0:T(8,128)(2,1)S(1)}, bf16[2,12,128,256]{3,2,1,0:T(8,128)(2,1)}, u32[]{:S(2)}) %copy-start) | copy-done | bytes 1572888
  15.0 0.0 copy-start.1
  15.0 0.0 copy-start.2
  15.0 0.5 turn_left.1.left_ref
  15.5 0.2 copy-done.1
  15.7 0.0 copy-done.2
  15.7 0.1 multiply_reduce_fusion
  15.8 0.1 fusion.2
  15.9 3.7 %all-to-all-done = bf16[16,48,128]{2,1,0:T(8,128)(2,1)S(1)} async-done(((bf16[16,48,128]{2,1,0:T(8,128)(2,1)}), bf16[16,48,128]{2,1,0:T(8,128)(2,1)S(1)}, u32[]{:S(2)}, u32[]{:S(2)}) %all-to-all-start) | async-done | bytes 196640 | tf_op jit(solution)/shard_map/all_to_all | solution.py:133
  19.5 2.0 %partial_tile.1 = bf16[256,1024]{1,0:T(8,128)(2,1)S(1)} custom-call(bf16[512,1536]{1,0:T(8,128)(2,1)S(1)} %turn_left.1.left_ref, bf16[768,128]{1,0:T(8,128)(2,1)S(1)} %bitcast.8, f32[16,128]{1,0:T(8,128)S(1)} %get-tuple-element.6.cos_ref, f32[16,128]{1,0:T(8,128)S(1)} %get-tuple-element.5.sin_ref), custom_call_target="tpu_custom_call" | custom-call | tf_op jit(solution)/shard_map/partial_tile/pallas_call | solution.py:89
  21.5 24.5 %all_to_all.10.a = bf16[32,8,1024]{2,1,0:T(8,128)(2,1)S(1)} all-to-all(bf16[32,8,1024]{2,1,0:T(8,128)(2,1)S(1)} %bitcast.6), channel_id=1, replica_groups={{352,416,480,48,112,176,240,304,368,432,496,0,64,128,192,256,320,384,44..., dimensions={0} | all-to-all | bytes 1048576 | tf_op jit(solution)/shard_map/all_to_all | solution.py:140
  46.1 1.0 %owned_sum.1 = f32[8,16,2,32]{3,2,1,0:T(2,128)} custom-call(bf16[32,8,1024]{2,1,0:T(8,128)(2,1)S(1)} %all_to_all.10.a), custom_call_target="tpu_custom_call" | custom-call | tf_op jit(solution)/shard_map/owned_sum/pallas_call | solution.py:115
Async XLA Ops:
  1.4 18.1 %all-to-all-start = ((bf16[16,48,128]{2,1,0:T(8,128)(2,1)}), bf16[16,48,128]{2,1,0:T(8,128)(2,1)S(1)}, u32[]{:S(2)}, u32[]{:S(2)}) async-start(bf16[16,48,128]{2,1,0:T(8,128)(2,1)} %broadcast_in_dim.10), calls=%async_computation | async-start | bytes 393216 | tf_op jit(solution)/shard_map/all_to_all | solution.py:133
  13.6 1.4 %copy-start = (bf16[2,12,128,256]{3,2,1,0:T(8,128)(2,1)S(1)}, bf16[2,12,128,256]{3,2,1,0:T(8,128)(2,1)}, u32[]{:S(2)}) copy-start(bf16[2,12,128,256]{3,2,1,0:T(8,128)(2,1)} %param.4) | copy-start | bytes 4718596
  15.0 0.7 %copy-start.1 = (s32[3,128]{1,0:T(4,128)S(1)}, s32[3,128]{1,0:T(4,128)}, u32[]{:S(2)}) copy-start(s32[3,128]{1,0:T(4,128)} %param.7) | copy-start | bytes 4612
  15.0 0.7 %copy-start.2 = (s32[16,3]{0,1:T(4,128)S(1)}, s32[16,3]{0,1:T(4,128)}, u32[]{:S(2)}) copy-start(s32[16,3]{0,1:T(4,128)} %param.6) | copy-start | bytes 580

commit v5 on v4

v5 whole, which is shorter than its diff:
```python
import functools
import math

import jax
import jax.numpy as jnp
from jax import lax
from jax.experimental import pallas as pl
from jax.experimental.pallas import tpu as pltpu
from jax.sharding import PartitionSpec as P

EXTENT = 96


def counted_from(first, members):
    start = members.index(first)
    return members[start:] + members[:start]


GROUP = 8
VMEM_LIMIT = 24 << 20
MODE_ORDER = [8 * h + 2 * x + c for h in (1, 0) for c in (1, 0) for x in (3, 2, 1, 0)]
SPACE_ORDER = counted_from(22, [4 * y + z for z in range(4) for y in range(8)])


def opening_kernel(own_hbm, momenta_hbm, coords_hbm, out_ref, cos_ref, sin_ref, own_ref, momenta_ref, coords_ref, turns_ref, sems):
    moves = [
        pltpu.make_async_copy(source, target, sems.at[k])
        for k, (source, target) in enumerate(
            ((own_hbm, own_ref), (momenta_hbm, momenta_ref), (coords_hbm, coords_ref))
        )
    ]
    for move in moves:
        move.start()
    for move in moves:
        move.wait()
    for k in range(out_ref.shape[0]):
        out_ref[k] = own_ref[...]
    dims, momenta = momenta_ref.shape
    for p in range(momenta):
        turns_ref[p : p + 1, :] = sum(momenta_ref[d : d + 1, p : p + 1] * coords_ref[d : d + 1, :] for d in range(dims))
    angles = jnp.mod(turns_ref[...], EXTENT).astype(jnp.float32) * (2.0 * math.pi / EXTENT)
    cos_ref[...] = jnp.cos(angles)
    sin_ref[...] = jnp.sin(angles)


def opening(own, momenta, coords, count):
    hbm, vmem = pl.BlockSpec(memory_space=pltpu.HBM), pl.BlockSpec(memory_space=pltpu.VMEM)
    phases = jax.ShapeDtypeStruct((momenta.shape[1], coords.shape[1]), jnp.float32)
    return pl.pallas_call(
        opening_kernel,
        out_shape=(jax.ShapeDtypeStruct((count,) + own.shape, own.dtype), phases, phases),
        in_specs=[hbm] * 3,
        out_specs=(vmem,) * 3,
        scratch_shapes=[
            pltpu.VMEM(own.shape, own.dtype),
            pltpu.VMEM(momenta.shape, momenta.dtype),
            pltpu.VMEM(coords.shape, coords.dtype),
            pltpu.VMEM(phases.shape, jnp.int32),
            pltpu.SemaphoreType.DMA((3,)),
        ],
        compiler_params=pltpu.CompilerParams(vmem_limit_bytes=8 << 20),
        name="opening",
    )(*(pltpu.with_memory_space_constraint(x, pltpu.HBM) for x in (own, momenta, coords)))


def partial_kernel(
    order, space_order, left_hbm, right_ref, cos_ref, sin_ref, out_ref, left_ref, plain_ref, rows_ref, sems
):
    moves = [pltpu.make_async_copy(left_hbm.at[k], left_ref.at[k], sems.at[k]) for k in range(2)]
    for move in moves:
        move.start()
    momenta, sites = cos_ref.shape
    depth, columns = left_ref.shape[1:]
    comps = depth // sites
    modes = right_ref.shape[0] // (2 * comps)
    half = GROUP * modes
    part = right_ref.shape[0] // len(order)
    for k, member in enumerate(order):
        plain_ref[member * part : (member + 1) * part, :] = right_ref[k * part : (k + 1) * part, :].astype(jnp.float32)
    rows = columns // len(space_order)
    groups = momenta // GROUP
    for q in range(groups):
        for c in range(comps):
            real = plain_ref[pl.ds(2 * c, modes, stride=2 * comps), :]
            imag = plain_ref[pl.ds(2 * c + 1, modes, stride=2 * comps), :]
            lanes = slice(c * sites, (c + 1) * sites)
            for k in range(GROUP):
                p = q * GROUP + k
                cos_row, sin_row = cos_ref[p : p + 1, :], sin_ref[p : p + 1, :]
                turned_re = (cos_row * real + sin_row * imag).astype(jnp.bfloat16)
                turned_im = (cos_row * imag - sin_row * real).astype(jnp.bfloat16)
                rows_ref[q, k * modes : (k + 1) * modes, lanes] = turned_re
                rows_ref[q, half + k * modes : half + (k + 1) * modes, lanes] = turned_im
    moves[0].wait()
    with_re = [jnp.dot(rows_ref[q], left_ref[0], preferred_element_type=jnp.float32) for q in range(groups)]
    moves[1].wait()
    for q in range(groups):
        with_im = jnp.dot(rows_ref[q], left_ref[1], preferred_element_type=jnp.float32)
        base = q * 2 * half
        for start, value in (
            (base, with_re[q][:half] + with_im[half:]),
            (base + half, with_re[q][half:] - with_im[:half]),
        ):
            tile = value.T
            tile = jnp.concatenate([tile[member * rows : (member + 1) * rows] for member in space_order], axis=0)
            out_ref[:, start : start + half] = tile.astype(out_ref.dtype)


def partial_tile(left, right, cosines, sines, order, space_order):
    rows, sites = right.shape
    _, depth, columns = left.shape
    modes = rows * sites // (2 * depth)
    count = cosines.shape[0]
    vmem = pl.BlockSpec(memory_space=pltpu.VMEM)
    return pl.pallas_call(
        functools.partial(partial_kernel, order, space_order),
        out_shape=jax.ShapeDtypeStruct((columns, count * 2 * modes), jnp.bfloat16),
        in_specs=[pl.BlockSpec(memory_space=pltpu.HBM), vmem, vmem, vmem],
        out_specs=vmem,
        scratch_shapes=[
            pltpu.VMEM(left.shape, left.dtype),
            pltpu.VMEM((rows, sites), jnp.float32),
            pltpu.VMEM((count // GROUP, 2 * GROUP * modes, depth), jnp.bfloat16),
            pltpu.SemaphoreType.DMA((2,)),
        ],
        compiler_params=pltpu.CompilerParams(vmem_limit_bytes=VMEM_LIMIT),
        name="partial_tile",
    )(pltpu.with_memory_space_constraint(left, pltpu.HBM), right, cosines, sines)


def sum_kernel(scale, pieces_ref, out_ref):
    _, momenta, parts, modes = out_ref.shape
    total = jnp.sum(pieces_ref[...].astype(jnp.float32), axis=0) * scale
    for p in range(momenta):
        for part in range(parts):
            group, k = divmod(p, GROUP)
            start = ((group * parts + part) * GROUP + k) * modes
            out_ref[:, p, part, :] = total[:, start : start + modes]


def owned_sum(pieces, momenta, scale):
    _, rows, width = pieces.shape
    return pl.pallas_call(
        lambda a, b: sum_kernel(scale, a, b),
        out_shape=jax.ShapeDtypeStruct((rows, momenta, 2, width // (2 * momenta)), jnp.float32),
        in_specs=[pl.BlockSpec(memory_space=pltpu.VMEM)],
        out_specs=pl.BlockSpec(memory_space=pltpu.VMEM),
        compiler_params=pltpu.CompilerParams(vmem_limit_bytes=8 << 20),
        name="owned_sum",
    )(pieces)


def body(left_modes, right_modes, momenta, coords):
    space, mode = lax.axis_size("space"), lax.axis_size("mode")
    held, _, comps, sites = right_modes.shape
    columns = left_modes.shape[-1]
    norm_scale = 1.0 / math.sqrt(comps * sites * space)
    own = right_modes.transpose(0, 2, 1, 3).reshape(held * comps * 2, sites)
    order, space_order = MODE_ORDER, SPACE_ORDER
    copies, cosines, sines = opening(own, momenta.T, coords, mode)
    right = lax.all_to_all(copies, "mode", 0, 0, axis_index_groups=[order], tiled=True)
    rows = columns // space
    left = left_modes.reshape(2, comps * sites, columns)
    tile = partial_tile(left, right.reshape(-1, sites), cosines, sines, order, space_order)
    pieces = tile.reshape(space, rows, tile.shape[1])
    owned = lax.all_to_all(
        pieces, "space", 0, 0, axis_index_groups=[space_order], tiled=True
    )
    return owned_sum(owned, momenta.shape[0], norm_scale)


def solution(mesh):
    in_specs = (
        P(None, None, "space", "mode"),
        P("mode", None, None, "space"),
        P(),
        P(None, "space"),
    )
    out_specs = P(("mode", "space"), None, None, None)
    return jax.shard_map(body, mesh=mesh, in_specs=in_specs, out_specs=out_specs, check_vma=False)
```

time: 47.6 us -> 47.6 us (level)
  blocking collectives: 24.5 us -> 42 us
  starting transfers between devices: 12.2 us -> 0 us
  waiting for transfers between devices: 3.66 us -> 0 us
  local copies, waits for them, and re-layouts: 3.04 us -> 0 us
  Pallas kernels: 3.44 us -> 5.16 us
    all_to_all x0 -> x1, blocking collectives: none -> 17.9 us  [body(): lax.all_to_all(copies, 'mode', 0, 0, axis_index_groups=[order], tiled=True)]
    all_to_all x1 -> x0, starting transfers between devices: 12.2 us -> none  [body(): lax.all_to_all(jnp.broadcast_to(own[None], (mode,) + own.shape), 'mode',...]
    all_to_all x1 -> x0, waiting for transfers between devices: 3.66 us -> none  [body(): lax.all_to_all(jnp.broadcast_to(own[None], (mode,) + own.shape), 'mode',...]
    pallas_call x2, Pallas kernels: 2.47 us -> 4.19 us  [the longest x1 3.24 us: partial_tile(): pl.pallas_call(functools.partial(partial_kernel, order, space_order), out...]
    unnamed x6 -> x0, local copies, waits for them, and re-layouts: 1.64 us -> none
    broadcast_in_dim x1 -> x0, local copies, waits for them, and re-layouts: 1.4 us -> none  [body(): jnp.broadcast_to(own[None], (mode,) + own.shape)]
  transfers between devices with their start and end apart: 1 -> 0, of which waited for: 1 -> 0; matrix products, arithmetic and copies ran while one was open for 0% -> 0% of each run, Pallas kernels for 1% -> 0%
where the time goes in v5:
time: 47.6 us; the launch traced here: 47.2 us
  blocking collectives  42 us (88%)
  Pallas kernels  5.16 us (11%)
    all_to_all x1, blocking collectives, body(): lax.all_to_all(pieces, 'space', 0, 0, axis_index_groups=[space_order], ti...  24.1 us
    all_to_all x1, blocking collectives, body(): lax.all_to_all(copies, 'mode', 0, 0, axis_index_groups=[order], tiled=True)  17.9 us
    pallas_call x1, Pallas kernels, partial_tile(): pl.pallas_call(functools.partial(partial_kernel, order, space_order), out...  3.24 us
    pallas_call x1, Pallas kernels, owned_sum(): pl.pallas_call(lambda a, b: sum_kernel(scale, a, b), out_shape=jax.ShapeD...  0.97 us

profile of v5, /device:TPU:6, one launch (start us, length us, event | category | flops | bytes accessed | tf_op | source)
XLA Modules:
  0.0 47.2 jit_solution(1571079269914689406)
XLA Ops:
  0.0 0.9 %opening.1 = (bf16[16,48,128]{2,1,0:T(8,128)(2,1)S(1)}, f32[16,128]{1,0:T(8,128)S(1)}, f32[16,128]{1,0:T(8,128)S(1)}) custom-call(bf16[48,128]{1,0:T(8,128)(2,1)} %bitcast.10, s32[3,16]{1,0:T(4,128)} %bitcast.11, s32[3,128]{1,0:T(4,128)} %coords_hbm.1), custom_call_target="tpu_custom_call" | custom-call | tf_op jit(solution)/shard_map/opening/pallas_call | solution.py:49
  1.0 17.9 %all_to_all.10 = bf16[16,48,128]{2,1,0:T(8,128)(2,1)S(1)} all-to-all(bf16[16,48,128]{2,1,0:T(8,128)(2,1)S(1)} %get-tuple-element.8), channel_id=1, replica_groups={{15,13,11,9,14,12,10,8,7,5,3,1,6,4,2,0},{31,29,27,25,30,28,26,24,23,21,..., dimensions={0} | all-to-all | bytes 393216 | tf_op jit(solution)/shard_map/all_to_all | solution.py:161
  18.9 3.2 %partial_tile.1 = bf16[256,1024]{1,0:T(8,128)(2,1)S(1)} custom-call(bf16[2,1536,256]{2,1,0:T(8,128)(2,1)} %bitcast.9, bf16[768,128]{1,0:T(8,128)(2,1)S(1)} %bitcast.8, f32[16,128]{1,0:T(8,128)S(1)} %get-tuple-element.9.cos_ref, f32[16,128]{1,0:T(8,128)S(1)} %get-tuple-element.10.sin_ref), custom_call_target="tpu_custom_call" | custom-call | tf_op jit(solution)/shard_map/partial_tile/pallas_call | solution.py:115
  22.1 24.1 %all_to_all.11.a = bf16[32,8,1024]{2,1,0:T(8,128)(2,1)S(1)} all-to-all(bf16[32,8,1024]{2,1,0:T(8,128)(2,1)S(1)} %bitcast.7), channel_id=1, replica_groups={{352,416,480,48,112,176,240,304,368,432,496,0,64,128,192,256,320,384,44..., dimensions={0} | all-to-all | bytes 1048576 | tf_op jit(solution)/shard_map/all_to_all | solution.py:166
  46.2 1.0 %owned_sum.1 = f32[8,16,2,32]{3,2,1,0:T(2,128)} custom-call(bf16[32,8,1024]{2,1,0:T(8,128)(2,1)S(1)} %all_to_all.11.a), custom_call_target="tpu_custom_call" | custom-call | tf_op jit(solution)/shard_map/owned_sum/pallas_call | solution.py:143
